TPU v7x, 32 devices: a whole 2x2x4 slice. The times are simulated.
32 devices in a mesh: batch: 8 (over y, x, core), tile: 4 (over z).
Axes of the slice: x: 2, y: 2, z: 4, core: 2. Of those that a mesh axis runs over, the one named last changes fastest.
Arguments:
- object_field: float32 [2, 2, 3072, 1536], P(None, None, 'batch', 'tile'), may hold values from -6 to 6
- probe_wave: bfloat16 [2, 256, 256], replicated, may hold values from -4.1875 to 4.1875
- intensities: float32 [512, 256, 256], P(('batch', 'tile')), may hold values from 0 to 4
- owner_rows: int32 [512, 1], P(('batch', 'tile')), may hold values from 0 to 7; in each aligned block of 16 rows (0 to 15, 16 to 31, ...) at most 4 rows name the same one
- offsets: int32 [512, 2], P(('batch', 'tile')), may hold values from 0 to 128
Outputs:
- new_object: float32 [2, 2, 3072, 1536], P(None, None, 'batch', 'tile')
- new_probe: float32 [2, 256, 256], replicated
Inputs may be any that keep to these rules, and one draw needn't show every extreme that they name: `owner_rows`: within the 16 positions of one device, each tile row is named at most 4 times.
All inputs are finite; a program needn't handle non-finite values.
Results may differ from a plain program's by a relative error of at most 0.008.
The roundings to bfloat16 on the way count: a program that leaves them out, or rounds other values in their place, can miss the bound.
Values may be sent and summed in bfloat16 or wider, within the bound.
A program may use at most 192 MiB of HBM per device.

v0:
```python
import math
import jax
import jax.numpy as jnp
from jax import lax
from jax.sharding import PartitionSpec as P

update_rate = 0.1
tv_weight = 12.0
tv_smooth = 1.0
probe_rate = 0.04


def extended(x, sides, width):
    for axis, dim in sides:
        size, length = (lax.axis_size(axis), x.shape[dim])
        up = [(i, (i + 1) % size) for i in range(size)]
        down = [(j, i) for i, j in up]
        last = lax.slice_in_dim(x, length - width, length, axis=dim)
        first = lax.slice_in_dim(x, 0, width, axis=dim)
        before = lax.ppermute(last, axis, up)
        after = lax.ppermute(first, axis, down)
        x = jnp.concatenate([before, x, after], axis=dim)
    return x


def tables(extent):
    counter = jnp.arange(extent, dtype=jnp.int32)
    product = counter[:, None] * counter[None, :] % extent
    angles = product.astype(jnp.float32) * (2.0 * math.pi / extent)
    scaling = 1.0 / math.sqrt(extent)
    cos_table = (jnp.cos(angles) * scaling).astype(jnp.bfloat16)
    sin_table = (-jnp.sin(angles) * scaling).astype(jnp.bfloat16)
    frequency = (counter + extent // 2) % extent - extent // 2
    squared = (frequency * frequency).astype(jnp.float32)
    phases = -(0.5 / extent) * (squared[:, None] + squared[None, :])
    return (cos_table, sin_table, jnp.cos(phases), jnp.sin(phases))


def transform(real_part, imag_part, cos_table, sin_table):
    extent = real_part.shape[0]
    left_stack = jnp.concatenate([cos_table, sin_table], 0)
    right_stack = jnp.concatenate([real_part, imag_part], 1)
    blocks = jnp.dot(left_stack, right_stack, preferred_element_type=jnp.float32)
    mid_real = (blocks[:extent, :extent] - blocks[extent:, extent:]).astype(jnp.bfloat16)
    mid_imag = (blocks[:extent, extent:] + blocks[extent:, :extent]).astype(jnp.bfloat16)
    left_two = jnp.concatenate([mid_real, mid_imag], 0)
    right_two = jnp.concatenate([cos_table, sin_table], 1)
    second = jnp.dot(left_two, right_two, preferred_element_type=jnp.float32)
    out_real = second[:extent, :extent] - second[extent:, extent:]
    out_imag = second[:extent, extent:] + second[extent:, :extent]
    return (out_real, out_imag)


def multislice(object_patch, probe_wave, measured, cos_table, sin_table, prop_real, prop_imag):
    slices = object_patch.shape[0]
    back_sin = -sin_table
    psi_real = probe_wave[0]
    psi_imag = probe_wave[1]
    entering = []
    for slab_index in range(slices):
        trans_real = object_patch[slab_index, 0].astype(jnp.float32)
        trans_imag = object_patch[slab_index, 1].astype(jnp.float32)
        entering.append((psi_real, psi_imag))
        wave_real = psi_real.astype(jnp.float32)
        wave_imag = psi_imag.astype(jnp.float32)
        prod_real = (wave_real * trans_real - wave_imag * trans_imag).astype(jnp.bfloat16)
        prod_imag = (wave_real * trans_imag + wave_imag * trans_real).astype(jnp.bfloat16)
        if slab_index + 1 < slices:
            far_real, far_imag = transform(prod_real, prod_imag, cos_table, sin_table)
            kick_real = (prop_real * far_real - prop_imag * far_imag).astype(jnp.bfloat16)
            kick_imag = (prop_real * far_imag + prop_imag * far_real).astype(jnp.bfloat16)
            near_real, near_imag = transform(kick_real, kick_imag, cos_table, back_sin)
            psi_real = near_real.astype(jnp.bfloat16)
            psi_imag = near_imag.astype(jnp.bfloat16)
    exit_real, exit_imag = transform(prod_real, prod_imag, cos_table, sin_table)
    misfit = 0.5 * (exit_real * exit_real + exit_imag * exit_imag - measured)
    chi_real = (misfit * exit_real).astype(jnp.bfloat16)
    chi_imag = (misfit * exit_imag).astype(jnp.bfloat16)
    grad_real, grad_imag = transform(chi_real, chi_imag, cos_table, back_sin)
    object_grads = [None] * slices
    for slab_index in reversed(range(slices)):
        trans_real = object_patch[slab_index, 0].astype(jnp.float32)
        trans_imag = object_patch[slab_index, 1].astype(jnp.float32)
        wave_real = entering[slab_index][0].astype(jnp.float32)
        wave_imag = entering[slab_index][1].astype(jnp.float32)
        object_grads[slab_index] = jnp.stack(
            [
                grad_real * wave_real + grad_imag * wave_imag,
                grad_imag * wave_real - grad_real * wave_imag,
            ]
        )
        dpsi_real = grad_real * trans_real + grad_imag * trans_imag
        dpsi_imag = grad_imag * trans_real - grad_real * trans_imag
        if slab_index > 0:
            back_real, back_imag = transform(
                dpsi_real.astype(jnp.bfloat16), dpsi_imag.astype(jnp.bfloat16), cos_table, back_sin
            )
            turn_real = (prop_real * back_real + prop_imag * back_imag).astype(jnp.bfloat16)
            turn_imag = (prop_real * back_imag - prop_imag * back_real).astype(jnp.bfloat16)
            grad_real, grad_imag = transform(turn_real, turn_imag, cos_table, sin_table)
    patch_grad = jnp.stack(object_grads).astype(jnp.bfloat16)
    probe_grad = jnp.stack([dpsi_real, dpsi_imag])
    return (patch_grad, probe_grad)


def tv_local(padded):
    corner_cells = padded[:, :, :-1, :-1]
    down_diff = padded[:, :, 1:, :-1] - corner_cells
    right_diff = padded[:, :, :-1, 1:] - corner_cells
    weight = 1.0 / jnp.sqrt(
        jnp.sum(down_diff * down_diff + right_diff * right_diff, axis=1, keepdims=True) + tv_smooth
    )
    flow_down = weight * down_diff
    flow_right = weight * right_diff
    return (
        flow_down[:, :, :-1, 1:]
        + flow_right[:, :, 1:, :-1]
        - flow_down[:, :, 1:, 1:]
        - flow_right[:, :, 1:, 1:]
    )


def on_device(object_field, probe_wave, intensities, owner_rows, offsets):
    slices = object_field.shape[0]
    tile_rows = object_field.shape[2]
    extent = probe_wave.shape[-1]
    local_rows = intensities.shape[0]
    nbatch = lax.axis_size("batch")
    capacity = max(2, 2 * local_rows // nbatch)
    slots_all = nbatch * capacity
    patch_shape = (slices, 2, extent, extent)
    targets = owner_rows[:, 0]
    serial = jnp.arange(local_rows, dtype=jnp.int32)
    earlier = (targets[:, None] == targets[None, :]) & (serial[None, :] < serial[:, None])
    ranks = jnp.sum(earlier.astype(jnp.int32), axis=1)
    slot_of = targets * capacity + ranks
    request = (
        jnp.zeros((slots_all, 2), jnp.int32).at[slot_of].set(offsets).reshape(nbatch, capacity, 2)
    )
    wanted = lax.all_to_all(request, "batch", split_axis=0, concat_axis=0, tiled=True).reshape(
        slots_all, 2
    )
    anchor = jnp.zeros((), jnp.int32)
    column = lax.all_gather(object_field.astype(jnp.bfloat16), "batch", axis=2, tiled=True)

    def cut_column(target, corner):
        return lax.dynamic_slice(
            column, (anchor, anchor, target * tile_rows + corner[0], corner[1]), patch_shape
        )

    patches_here = jax.vmap(cut_column)(targets, offsets)
    cos_table, sin_table, prop_real, prop_imag = tables(extent)

    def visit_one(probe_local, inputs):
        object_patch, measured = inputs
        patch_grad, probe_grad = multislice(
            object_patch, probe_wave, measured, cos_table, sin_table, prop_real, prop_imag
        )
        return (probe_local + probe_grad, patch_grad)

    probe_local, patch_grads = lax.scan(
        visit_one, jnp.zeros((2, extent, extent), jnp.float32), (patches_here, intensities)
    )
    outgoing = jnp.zeros((slots_all,) + patch_shape, jnp.bfloat16).at[slot_of].set(patch_grads)
    outgoing = outgoing.reshape((nbatch, capacity) + patch_shape)
    returned = lax.all_to_all(outgoing, "batch", split_axis=0, concat_axis=0, tiled=True).reshape(
        (slots_all,) + patch_shape
    )

    def add_slot(slot_idx, field_grad):
        corner = wanted[slot_idx]
        start = (anchor, anchor, corner[0], corner[1])
        current = lax.dynamic_slice(field_grad, start, patch_shape)
        return lax.dynamic_update_slice(
            field_grad, current + returned[slot_idx].astype(jnp.float32), start
        )

    field_grad = lax.fori_loop(0, slots_all, add_slot, jnp.zeros(object_field.shape, jnp.float32))
    probe_total = lax.psum(probe_local, ("batch", "tile"))
    padded = extended(object_field, (("batch", 2), ("tile", 3)), 1)
    new_object = object_field - update_rate * (field_grad + tv_weight * tv_local(padded))
    new_probe = probe_wave.astype(jnp.float32) - probe_rate * probe_total
    return (new_object, new_probe)


def solution(mesh):
    return jax.shard_map(
        on_device,
        mesh=mesh,
        in_specs=(
            P(None, None, "batch", "tile"),
            P(),
            P(("batch", "tile"), None, None),
            P(("batch", "tile"), None),
            P(("batch", "tile"), None),
        ),
        out_specs=(P(None, None, "batch", "tile"), P()),
        check_vma=False,
    )
```

profile of v0, /device:TPU:6, one launch (start us, length us, event | category | flops | bytes accessed | tf_op | source)
XLA Modules:
  0.0 1374.3 jit_solution(8575923773611135377)
XLA Ops:
  18.4 51.1 %all-gather.2.cloned.1.call-done = bf16[2,2,3072,384]{3,2,1,0:T(8,128)(2,1)} async-done(((bf16[2,2,384,384]{3,2,1,0:T(8,128)(2,1)}), bf16[2,2,3072,384]{3,2,1,0:T(8,128)(2,1)}) %all-gather.2.cloned.1.call-update) | async-done | bytes 9437200 | tf_op jit(solution)/shard_map/all_gather | solution.py:144
  73.9 67.6 %while.33 = (s32[]{:T(128)}, bf16[2,2,3072,384]{3,2,1,0:T(8,128)(2,1)}, s32[16,4]{0,1:T(4,128)S(1)}, bf16[16,2,2,256,256]{4,3,2,1,0:T(8,128)(2,1)}, s32[]{:T(128)}) while((s32[]{:T(128)}, bf16[2,2,3072,384]{3,2,1,0:T(8,128)(2,1)}, s32[16,4]{0,1:T(4,128)S(1)}, bf16[16,2,2,256,256]{4,3,2,1,0:T(8,128)(2,1)}, s32[]{:T(128)}) %tuple.156), condition=%wide.while_cond, body=%wide.while_body.sunk | while | flops 2 | bytes 1050225 | solution.py:147
  145.7 224.0 %while.34 = (s32[]{:T(128)}, f32[2,256,256]{1,2,0:T(8,128)}, bf16[16,2,2,256,256]{4,3,2,1,0:T(8,128)(2,1)}, bf16[2,256,256]{1,2,0:T(8,128)(2,1)S(1)}, bf16[16,2,...) while((s32[]{:T(128)}, f32[2,256,256]{1,2,0:T(8,128)}, ...), condition=%wide.region_3.4_spmd.clone.clone.clone.clone, body=%wide.region_2.3_spmd.clone.clone.clone.clone.sunk | while | flops 1626800128 | bytes 54268612 | solution.py:161
  375.6 21.3 %scatter_fusion = bf16[32,2,2,256,256]{4,3,2,1,0:T(8,128)(2,1)} fusion(bf16[32,2,2,256,256]{4,3,2,1,0:T(8,128)(2,1)} %broadcast_in_dim.13, s32[16]{0:T(128)S(1)} %get-tuple-element.547, bf16[16,2,2,256,256]{4,3,2,1,0:T(8,128)(2,1)} %get-tuple-element.229), kind=kCustom, calls=%fused_computation.1 | custom fusion | bytes 25165888 | tf_op jit(solution)/shard_map/scatter | solution.py:164
  409.1 176.3 %collective-permute-done = f32[2,2,1,384]{3,1,2,0:T(2,128)S(1)} collective-permute-done((f32[2,2,1,384]{3,1,2,0:T(2,128)S(1)}, f32[2,2,1,384]{3,1,2,0:T(2,128)S(1)}, u32[]{:S(2)}, u32[]{:S(2)}) %collective-permute-start) | collective-permute-done | bytes 6176 | tf_op jit(solution)/shard_map/ppermute | solution.py:20
  613.5 123.8 %all-reduce.2.cloned.1.call-done = f32[2,256,256]{2,1,0:T(8,128)} async-done(((f32[2,256,256]{2,1,0:T(8,128)}), f32[2,256,256]{2,1,0:T(8,128)}) %all-reduce.2.cloned.1.call-update) | async-done | bytes 524304 | tf_op jit(solution)/shard_map/psum | solution.py:179
  740.7 617.0 %while.32 = (s32[]{:T(128)}, f32[2,2,384,384]{2,3,1,0:T(8,128)}, s32[32,2]{0,1:T(2,128)S(1)}, bf16[32,2,2,256,256]{4,3,2,1,0:T(8,128)(2,1)}, s32[]{:T(128)}, /*index=5*/s32[]{:T(128)}, s32[]{:T(128)}) while((s32[]{:T(128)}, f32[2,2,384,384]{2,3,1,0:T(8,128)}, s32[32,2]{0,1:T(2,128)S(1)}, bf16[32,2,2,256,256]{4,3,2,1,0:T(8,128)(2,1)}, ...), condition=%wide.region_6.7_spmd, body=%wide.region_5.6_spmd.sunk | while | flops 524296 | bytes 11010245 | solution.py:178
  767.6 11.1 dynamic_update_slice.20
  786.7 11.6 dynamic_update_slice.20
  844.2 11.1 dynamic_update_slice.20
  863.3 11.7 dynamic_update_slice.20
  901.9 11.7 dynamic_update_slice.20
  921.5 11.7 dynamic_update_slice.20
  941.1 11.6 dynamic_update_slice.20
  960.6 11.6 dynamic_update_slice.20
  999.1 11.4 dynamic_update_slice.20
  1018.4 11.1 dynamic_update_slice.20
  1037.5 11.2 dynamic_update_slice.20
  1056.6 11.7 dynamic_update_slice.20
  1076.2 11.1 dynamic_update_slice.20
  1095.2 11.5 dynamic_update_slice.20
  1133.6 11.2 dynamic_update_slice.20
  1152.7 11.6 dynamic_update_slice.20
  1172.2 11.1 dynamic_update_slice.20
  1191.3 11.7 dynamic_update_slice.20
  1229.9 11.6 dynamic_update_slice.20
  1249.4 11.6 dynamic_update_slice.20
  1268.9 11.2 dynamic_update_slice.20
  1288.0 11.7 dynamic_update_slice.20
  1307.6 11.4 dynamic_update_slice.20
  1326.9 11.7 dynamic_update_slice.20
  1346.5 11.2 dynamic_update_slice.20
  (971 shorter events, 580.4 us)
Async XLA Ops:
  7.2 2.9 copy-start.6
  7.2 3.0 copy-start.7
  7.2 8.8 copy-start.4
  7.2 62.3 %all-gather.2.cloned.1.call-start = ((), (), s32[]{:S(2)}) async-start(), calls=%async_computation.2 | async-start | bytes 10616832 | tf_op jit(solution)/shard_map/all_gather | solution.py:144
  11.8 385.2 %all-to-all-start = ((s32[8,4,2]{1,2,0:T(2,128)}), s32[8,4,2]{1,2,0:T(2,128)S(1)}, u32[]{:S(2)}, u32[]{:S(2)}) async-start(s32[8,4,2]{1,2,0:T(2,128)} %copy.81), calls=%async_computation | async-start | bytes 16384 | tf_op jit(solution)/shard_map/all_to_all | solution.py:140
  157.5 1.3 copy-start.1
  158.9 0.8 copy-start.2
  171.4 1.3 copy-start.1
  172.9 0.8 copy-start.2
  185.4 1.3 copy-start.1
  199.4 1.3 copy-start.1
  213.4 1.3 copy-start.1
  227.4 1.3 copy-start.1
  241.4 1.3 copy-start.1
  255.4 1.3 copy-start.1
  269.4 1.3 copy-start.1
  283.4 1.3 copy-start.1
  297.4 1.3 copy-start.1
  311.4 1.3 copy-start.1
  325.4 1.3 copy-start.1
  339.4 1.3 copy-start.1
  353.4 1.4 copy-start.1
  367.4 1.3 copy-start.1
  397.0 7.3 copy-start
  397.0 342.2 %all-to-all-start.1 = ((bf16[8,4,2,2,256,256]{5,4,3,2,1,0:T(8,128)(2,1)}), bf16[8,4,2,2,256,256]{5,4,3,2,1,0:T(8,128)(2,1)}, u32[]{:S(2)}, u32[]{:S(2)}) async-start(bf16[8,4,2,2,256,256]{5,4,3,2,1,0:T(8,128)(2,1)} %bitcast.219), calls=%async_computation.1 | async-start | bytes 33554432 | tf_op jit(solution)/shard_map/all_to_all | solution.py:166
  404.2 333.0 %all-reduce.2.cloned.1.call-start = ((), (), s32[]{:S(2)}) async-start(), calls=%async_computation.3 | async-start | bytes 1048576 | tf_op jit(solution)/shard_map/psum | solution.py:179
  404.3 181.1 %collective-permute-start = (f32[2,2,1,384]{3,1,2,0:T(2,128)S(1)}, f32[2,2,1,384]{3,1,2,0:T(2,128)S(1)}, u32[]{:S(2)}, u32[]{:S(2)}) collective-permute-start(f32[2,2,1,384]{3,1,2,0:T(2,128)S(1)} %copy.111), channel_id=1, source_target_pairs={{0,4},{4,8},{8,12},{12,16},{16,20},{20,24},{24,28},{28,0},{1,5},{5... | collective-permute-start | bytes 18440 | tf_op jit(solution)/shard_map/ppermute | solution.py:20
  404.4 181.4 %collective-permute-start.1 = (f32[2,2,1,384]{3,1,2,0:T(2,128)S(1)}, f32[2,2,1,384]{3,1,2,0:T(2,128)S(1)}, u32[]{:S(2)}, u32[]{:S(2)}) collective-permute-start(f32[2,2,1,384]{3,1,2,0:T(2,128)S(1)} %copy.112), channel_id=1, source_target_pairs={{4,0},{8,4},{12,8},{16,12},{20,16},{24,20},{28,24},{0,28},{5,1},{9... | collective-permute-start | bytes 18440 | tf_op jit(solution)/shard_map/ppermute | solution.py:21
  593.7 1.7 copy-start.3
  595.4 8.4 collective-permute-start.2
  596.9 6.9 collective-permute-start.3
  608.9 128.3 %copy-start.5 = (bf16[2,256,256]{2,1,0:T(8,128)(2,1)S(1)}, bf16[2,256,256]{2,1,0:T(8,128)(2,1)}, u32[]{:S(2)}) copy-start(bf16[2,256,256]{2,1,0:T(8,128)(2,1)} %param.10) | copy-start | bytes 786436
  (14 other events, 11.1 us)
Sparse Core Ops, SparseCore 0:
  10.5 58.9 all-gather.1
  609.0 128.1 all-reduce.1
where the time goes:
time: 1390 us; the launch traced here: 1370 us
  local copies, waits for them, and re-layouts  663 us (48%)
  waiting for transfers between devices  351 us (25%)
  other arithmetic  143 us (10%)
  loops' own time  121 us (9%)
  matrix products  64.9 us (5%)
  starting transfers between devices  17.1 us (1%)
  between operations  14.2 us (1%)
    dynamic_update_slice x64, local copies, waits for them, and re-layouts, add_slot(): lax.dynamic_update_slice(field_grad, current + returned[slot_idx].astype(...  374 us
    ppermute x2, waiting for transfers between devices, extended(): before = lax.ppermute(last, axis, up)  176 us
    psum x1, waiting for transfers between devices, on_device(): probe_total = lax.psum(probe_local, ('batch', 'tile'))  124 us
    another operation x1, loops' own time, on_device(): lax.fori_loop(0, slots_all, add_slot, jnp.zeros(object_field.shape, jnp.f...  118 us
    dynamic_slice x64, local copies, waits for them, and re-layouts, add_slot(): current = lax.dynamic_slice(field_grad, start, patch_shape)  67.6 us
    gather x48, local copies, waits for them, and re-layouts  67.5 us
    all_gather x1, waiting for transfers between devices, on_device(): lax.all_gather(object_field.astype(jnp.bfloat16), 'batch', axis=2, tiled=...  51.1 us
    dynamic_slice x64, local copies, waits for them, and re-layouts, on_device(): lax.scan(visit_one, jnp.zeros((2, extent, extent), jnp.float32), (patches...  49.4 us
  transfers between devices with their start and end apart: 8, of which 3 were waited for; matrix products, arithmetic and copies ran while one was open for 25% of the time, Pallas kernels for 0%

commit v1 on v0

--- a/solution.py
+++ b/solution.py
@@ -176,7 +176,7 @@
         )
 
     field_grad = lax.fori_loop(0, slots_all, add_slot, jnp.zeros(object_field.shape, jnp.float32))
-    probe_total = lax.psum(probe_local, ("batch", "tile"))
+    probe_total = jnp.sum(lax.all_gather(probe_local, ("batch", "tile")), axis=0)
     padded = extended(object_field, (("batch", 2), ("tile", 3)), 1)
     new_object = object_field - update_rate * (field_grad + tv_weight * tv_local(padded))
     new_probe = probe_wave.astype(jnp.float32) - probe_rate * probe_total

time: 1390 us -> 1320 us (0.950)
  waiting for transfers between devices: 351 us -> 272 us
    psum x1 -> x0, waiting for transfers between devices: 124 us -> none  [on_device(): probe_total = lax.psum(probe_local, ('batch', 'tile'))]
    ppermute x2, waiting for transfers between devices: 176 us -> 221 us  [extended(): before = lax.ppermute(last, axis, up)]
  transfers between devices with their start and end apart: 8 -> 8, of which waited for: 3 -> 2; matrix products, arithmetic and copies ran while one was open for 25% -> 66% of each run, Pallas kernels for 0% -> 0%
where the time goes in v1:
time: 1320 us; the launch traced here: 1300 us
  local copies, waits for them, and re-layouts  669 us (51%)
  waiting for transfers between devices  272 us (21%)
  other arithmetic  148 us (11%)
  loops' own time  118 us (9%)
  matrix products  64.9 us (5%)
  starting transfers between devices  16.6 us (1%)
  between operations  14.3 us (1%)
    dynamic_update_slice x64, local copies, waits for them, and re-layouts, add_slot(): lax.dynamic_update_slice(field_grad, current + returned[slot_idx].astype(...  376 us
    ppermute x2, waiting for transfers between devices, extended(): before = lax.ppermute(last, axis, up)  221 us
    another operation x1, loops' own time, on_device(): lax.fori_loop(0, slots_all, add_slot, jnp.zeros(object_field.shape, jnp.f...  114 us
    gather x48, local copies, waits for them, and re-layouts  67.6 us
    dynamic_slice x64, local copies, waits for them, and re-layouts, add_slot(): current = lax.dynamic_slice(field_grad, start, patch_shape)  67.6 us
    all_gather x1, waiting for transfers between devices, on_device(): lax.all_gather(object_field.astype(jnp.bfloat16), 'batch', axis=2, tiled=...  51.1 us
    dynamic_slice x64, local copies, waits for them, and re-layouts, on_device(): lax.scan(visit_one, jnp.zeros((2, extent, extent), jnp.float32), (patches...  49.4 us
    add x32, other arithmetic, add_slot(): current + returned[slot_idx].astype(jnp.float32)  37.6 us
  transfers between devices with their start and end apart: 8, of which 2 were waited for; matrix products, arithmetic and copies ran while one was open for 66% of the time, Pallas kernels for 0%

profile of v1, /device:TPU:6, one launch (start us, length us, event | category | flops | bytes accessed | tf_op | source)
XLA Modules:
  0.0 1302.4 jit_solution(5085279719609666951)
XLA Ops:
  18.4 51.1 %all-gather.4.cloned.1.call-done = bf16[2,2,3072,384]{3,2,1,0:T(8,128)(2,1)} async-done(((bf16[2,2,384,384]{3,2,1,0:T(8,128)(2,1)}), bf16[2,2,3072,384]{3,2,1,0:T(8,128)(2,1)}) %all-gather.4.cloned.1.call-update) | async-done | bytes 9437200 | tf_op jit(solution)/shard_map/all_gather | solution.py:144
  73.9 67.6 %while.33 = (s32[]{:T(128)}, bf16[2,2,3072,384]{3,2,1,0:T(8,128)(2,1)}, s32[16,4]{0,1:T(4,128)S(1)}, bf16[16,2,2,256,256]{4,3,2,1,0:T(8,128)(2,1)}, s32[]{:T(128)}) while((s32[]{:T(128)}, bf16[2,2,3072,384]{3,2,1,0:T(8,128)(2,1)}, s32[16,4]{0,1:T(4,128)S(1)}, bf16[16,2,2,256,256]{4,3,2,1,0:T(8,128)(2,1)}, s32[]{:T(128)}) %tuple.156), condition=%wide.while_cond, body=%wide.while_body.sunk | while | flops 2 | bytes 1050225 | solution.py:147
  145.8 224.1 %while.34 = (s32[]{:T(128)}, f32[2,256,256]{1,2,0:T(8,128)}, bf16[16,2,2,256,256]{4,3,2,1,0:T(8,128)(2,1)}, bf16[2,256,256]{1,2,0:T(8,128)(2,1)S(1)}, bf16[16,2,...) while((s32[]{:T(128)}, f32[2,256,256]{1,2,0:T(8,128)}, ...), condition=%wide.region_3.4_spmd.clone.clone.clone.clone, body=%wide.region_2.3_spmd.clone.clone.clone.clone.sunk | while | flops 1626800128 | bytes 54268612 | solution.py:161
  375.8 21.3 %scatter_fusion = bf16[32,2,2,256,256]{4,3,2,1,0:T(8,128)(2,1)} fusion(bf16[32,2,2,256,256]{4,3,2,1,0:T(8,128)(2,1)} %broadcast_in_dim.13, s32[16]{0:T(128)S(1)} %get-tuple-element.547, bf16[16,2,2,256,256]{4,3,2,1,0:T(8,128)(2,1)} %get-tuple-element.229), kind=kCustom, calls=%fused_computation.1 | custom fusion | bytes 25165888 | tf_op jit(solution)/shard_map/scatter | solution.py:164
  413.2 220.9 %collective-permute-done = f32[2,2,1,384]{3,1,2,0:T(2,128)S(1)} collective-permute-done((f32[2,2,1,384]{3,1,2,0:T(2,128)S(1)}, f32[2,2,1,384]{3,1,2,0:T(2,128)S(1)}, u32[]{:S(2)}, u32[]{:S(2)}) %collective-permute-start) | collective-permute-done | bytes 6176 | tf_op jit(solution)/shard_map/ppermute | solution.py:20
  659.3 615.8 %while.32 = (s32[]{:T(128)}, f32[2,2,384,384]{2,3,1,0:T(8,128)}, s32[32,2]{0,1:T(2,128)S(1)}, bf16[32,2,2,256,256]{4,3,2,1,0:T(8,128)(2,1)}, s32[]{:T(128)}, /*index=5*/s32[]{:T(128)}, s32[]{:T(128)}) while((s32[]{:T(128)}, f32[2,2,384,384]{2,3,1,0:T(8,128)}, s32[32,2]{0,1:T(2,128)S(1)}, bf16[32,2,2,256,256]{4,3,2,1,0:T(8,128)(2,1)}, ...), condition=%wide.region_6.7_spmd, body=%wide.region_5.6_spmd.sunk | while | flops 524296 | bytes 11010245 | solution.py:178
  686.1 11.2 dynamic_update_slice.20
  705.2 11.7 dynamic_update_slice.20
  724.7 11.2 dynamic_update_slice.20
  762.6 11.2 dynamic_update_slice.20
  781.7 11.7 dynamic_update_slice.20
  820.2 11.7 dynamic_update_slice.20
  839.7 11.7 dynamic_update_slice.20
  859.3 11.6 dynamic_update_slice.20
  878.7 11.6 dynamic_update_slice.20
  917.2 11.4 dynamic_update_slice.20
  936.4 11.2 dynamic_update_slice.20
  955.4 11.3 dynamic_update_slice.20
  974.6 11.7 dynamic_update_slice.20
  994.1 11.2 dynamic_update_slice.20
  1013.1 11.5 dynamic_update_slice.20
  1051.4 11.3 dynamic_update_slice.20
  1070.5 11.6 dynamic_update_slice.20
  1089.9 11.2 dynamic_update_slice.20
  1109.0 11.7 dynamic_update_slice.20
  1147.5 11.6 dynamic_update_slice.20
  1166.9 11.6 dynamic_update_slice.20
  1186.4 11.3 dynamic_update_slice.20
  1205.5 11.7 dynamic_update_slice.20
  1225.0 11.4 dynamic_update_slice.20
  1244.3 11.7 dynamic_update_slice.20
  1263.8 11.3 dynamic_update_slice.20
  (972 shorter events, 578.6 us)
Async XLA Ops:
  7.2 2.9 copy-start.5
  7.2 3.0 copy-start.6
  7.2 8.8 copy-start.4
  7.2 62.3 %all-gather.4.cloned.1.call-start = ((), (), s32[]{:S(2)}) async-start(), calls=%async_computation.2 | async-start | bytes 10616832 | tf_op jit(solution)/shard_map/all_gather | solution.py:144
  11.8 385.3 %all-to-all-start = ((s32[8,4,2]{1,2,0:T(2,128)}), s32[8,4,2]{1,2,0:T(2,128)S(1)}, u32[]{:S(2)}, u32[]{:S(2)}) async-start(s32[8,4,2]{1,2,0:T(2,128)} %copy.85), calls=%async_computation | async-start | bytes 16384 | tf_op jit(solution)/shard_map/all_to_all | solution.py:140
  157.5 1.3 copy-start
  159.0 0.8 copy-start.1
  171.5 1.3 copy-start
  173.0 0.8 copy-start.1
  185.5 1.3 copy-start
  199.5 1.3 copy-start
  213.5 1.3 copy-start
  227.5 1.3 copy-start
  228.9 0.8 copy-start.1
  241.4 1.3 copy-start
  255.4 1.3 copy-start
  269.5 1.3 copy-start
  283.5 1.3 copy-start
  297.5 1.3 copy-start
  311.5 1.3 copy-start
  325.5 1.3 copy-start
  339.5 1.3 copy-start
  353.5 1.3 copy-start
  367.5 1.4 copy-start
  397.0 7.2 copy-start.2
  397.0 260.7 %all-to-all-start.1 = ((bf16[8,4,2,2,256,256]{5,4,3,2,1,0:T(8,128)(2,1)}), bf16[8,4,2,2,256,256]{5,4,3,2,1,0:T(8,128)(2,1)}, u32[]{:S(2)}, u32[]{:S(2)}) async-start(bf16[8,4,2,2,256,256]{5,4,3,2,1,0:T(8,128)(2,1)} %bitcast.220), calls=%async_computation.1 | async-start | bytes 33554432 | tf_op jit(solution)/shard_map/all_to_all | solution.py:166
  404.3 883.1 %all-gather.6.cloned.1.call-start = ((), (), s32[]{:S(2)}) async-start(), calls=%async_computation.3 | async-start | bytes 17301504 | tf_op jit(solution)/shard_map/all_gather | solution.py:179
  406.1 228.0 %collective-permute-start = (f32[2,2,1,384]{3,1,2,0:T(2,128)S(1)}, f32[2,2,1,384]{3,1,2,0:T(2,128)S(1)}, u32[]{:S(2)}, u32[]{:S(2)}) collective-permute-start(f32[2,2,1,384]{3,1,2,0:T(2,128)S(1)} %copy.119), channel_id=1, source_target_pairs={{0,4},{4,8},{8,12},{12,16},{16,20},{20,24},{24,28},{28,0},{1,5},{5... | collective-permute-start | bytes 18440 | tf_op jit(solution)/shard_map/ppermute | solution.py:20
  406.3 228.2 %collective-permute-start.1 = (f32[2,2,1,384]{3,1,2,0:T(2,128)S(1)}, f32[2,2,1,384]{3,1,2,0:T(2,128)S(1)}, u32[]{:S(2)}, u32[]{:S(2)}) collective-permute-start(f32[2,2,1,384]{3,1,2,0:T(2,128)S(1)} %copy.120), channel_id=1, source_target_pairs={{4,0},{8,4},{12,8},{16,12},{20,16},{24,20},{28,24},{0,28},{5,1},{9... | collective-permute-start | bytes 18440 | tf_op jit(solution)/shard_map/ppermute | solution.py:21
  641.8 1.7 copy-start.3
  643.4 9.0 collective-permute-start.3
  646.8 5.7 collective-permute-start.2
  (13 other events, 10.3 us)
Sparse Core Ops, SparseCore 0:
  10.5 58.9 all-gather.3
  408.6 231.8 all-gather.5
